TPU v7x, 256 devices: a whole 4x4x8 slice. The times are simulated.
256 devices in a mesh: section: 8 (over z), neuron: 32 (over y, x, core).
Axes of the slice: x: 4, y: 4, z: 8, core: 2. Of those that a mesh axis runs over, the one named last changes fastest.
Arguments:
- inputs: bfloat16 [2, 256, 65536], P(None, None, 'neuron'), may hold values from -6 to 6
- weights: bfloat16 [16, 512, 3, 128, 128], P('section', 'neuron'), may hold values from -0.4375 to 0.4375
- bias: bfloat16 [16, 65536], P('section', 'neuron'), may hold values from -0.19921875 to 0.19921875
- offsets: int32 [16, 3], P('section'), may hold values from -3 to 3, as said below
Outputs:
- outputs: bfloat16 [2, 256, 65536], P(None, 'section', 'neuron')
Inputs may be any that keep to these rules, and one draw needn't show every extreme that they name: `offsets`: band 0 has offset 0; band 1 lies in 1 .. 3 and band 2 in -3 .. -1; some layer has 3 in band 1 and some layer -3 in band 2.
All inputs are finite; a program needn't handle non-finite values.
Results may differ from a plain program's by a relative error of at most 0.029.
Values may be sent and summed in bfloat16 or wider, within the bound.
A program may use at most 128 MiB of HBM per device.

v0:
```python
import jax
import jax.numpy as jnp
from jax import lax
from jax.sharding import PartitionSpec as P

HALO = 3
ceiling = 2.0


def padded(block, sides, width):
    for axis, dim in sides:
        count = lax.axis_size(axis)
        forward = [(i, i + 1) for i in range(count - 1)]
        forward.append((count - 1, 0))
        backward = [(target, source) for source, target in forward]
        low = lax.ppermute(
            lax.slice_in_dim(block, block.shape[dim] - width, None, axis=dim), axis, forward
        )
        high = lax.ppermute(lax.slice_in_dim(block, 0, width, axis=dim), axis, backward)
        block = jnp.concatenate([low, block, high], axis=dim)
    return block


def from_behind(value, axis, steps):
    count = lax.axis_size(axis)
    first, last = (max(0, -steps), min(count, count - steps))
    return lax.ppermute(value, axis, [(source, source + steps) for source in range(first, last)])


def spread(value, axis, source):
    kept = jnp.where(lax.axis_index(axis) == source, value, 0).astype(value.dtype)
    return lax.psum(kept, axis)


def shards(inputs, weights, bias, offsets):
    sections = lax.axis_size("section")
    section_index = lax.axis_index("section")
    micro_count, row_count, local_width = inputs.shape
    layer_count, block_count, band_count, block_size = (
        weights.shape[0],
        weights.shape[1],
        weights.shape[2],
        weights.shape[3],
    )
    packed = jnp.concatenate(
        [
            weights.reshape(layer_count, block_count, band_count * block_size, block_size),
            bias.reshape(layer_count, block_count, 1, block_size),
        ],
        axis=2,
    )
    table_edge = (packed.shape[1] - block_count) // 2

    def apply_layer(extended, table, layer_offsets, layer, margin):
        rows_here = extended.shape[0]
        out_blocks = block_count + 2 * margin
        first = table_edge - margin
        layer_weights = table[layer, first : first + out_blocks]
        summed = jnp.zeros((rows_here, out_blocks, block_size), jnp.float32)
        for band_index in range(band_count):
            start_col = (HALO + layer_offsets[layer, band_index]) * block_size
            shifted = lax.dynamic_slice_in_dim(
                extended, start_col, out_blocks * block_size, 1
            ).reshape(rows_here, out_blocks, block_size)
            block_weights = layer_weights[
                :, band_index * block_size : (band_index + 1) * block_size
            ]
            summed = summed + jnp.einsum(
                "rjk,jkn->rjn", shifted, block_weights, preferred_element_type=jnp.float32
            )
        bias_rows = layer_weights[:, band_count * block_size].astype(jnp.float32)
        preact = summed + bias_rows[None]
        return (
            jnp.clip(preact, 0.0, ceiling)
            .astype(jnp.bfloat16)
            .reshape(rows_here, out_blocks * block_size)
        )

    def run_section(current, table, layer_offsets):
        for layer in range(layer_count):
            extended = padded(current, (("neuron", 1),), HALO * block_size)
            current = apply_layer(extended, table, layer_offsets, layer, 0)
        return current

    share_rows = row_count // sections

    def advance(step_index, carry):
        incoming, finished_rows = carry
        arriving = lax.dynamic_index_in_dim(
            inputs, jnp.minimum(step_index, micro_count - 1), 0, keepdims=False
        )
        current = jnp.where(section_index == 0, arriving, incoming)
        produced = run_section(current, packed, offsets)
        slot_index = jnp.clip(step_index - (sections - 1), 0, micro_count - 1)
        finished = jnp.logical_and(section_index == sections - 1, step_index >= sections - 1)
        previous = lax.dynamic_index_in_dim(finished_rows, slot_index, 0, keepdims=False)
        finished_rows = lax.dynamic_update_index_in_dim(
            finished_rows, jnp.where(finished, produced, previous), slot_index, 0
        )
        incoming = from_behind(produced, "section", 1)
        return (incoming, finished_rows)

    initial = (
        jnp.zeros((row_count, local_width), jnp.bfloat16),
        jnp.zeros((micro_count, row_count, local_width), jnp.bfloat16),
    )
    incoming, finished_rows = lax.fori_loop(0, micro_count + sections - 1, advance, initial)
    everything = spread(finished_rows, "section", sections - 1)
    return lax.dynamic_slice_in_dim(everything, section_index * share_rows, share_rows, 1)


def solution(mesh):
    in_specs = (
        P(None, None, "neuron"),
        P("section", "neuron", None, None, None),
        P("section", "neuron"),
        P("section", None),
    )
    out_specs = P(None, "section", "neuron")
    return jax.shard_map(shards, mesh=mesh, in_specs=in_specs, out_specs=out_specs, check_vma=False)
```

profile of v0, /device:TPU:2, one launch (start us, length us, event | category | flops | bytes accessed | tf_op | source)
XLA Modules:
  0.0 552.5 jit_solution(16289615240674995746)
XLA Ops:
  22.6 429.7 %while.17 = (s32[]{:T(128)}, bf16[256,2048]{0,1:T(8,128)(2,1)}, bf16[2,256,2048]{2,1,0:T(8,128)(2,1)}, pred[]{:T(512)}, bf16[2,256,2048]{2,1,0:T(8,128)(2,1)}, /...) while((s32[]{:T(128)}, bf16[256,2048]{0,1:T(8,128)(2,1)}, ...), condition=%wide.region_1.2_spmd, body=%wide.region_0.1_spmd.sunk | while | flops 820252672 | bytes 80798200 | solution.py:107
  36.4 7.6 %collective-permute-done.3 = bf16[256,384]{0,1:T(8,128)(2,1)S(1)} collective-permute-done((bf16[256,384]{0,1:T(8,128)(2,1)S(1)}, bf16[256,384]{0,1:T(8,128)(2,1)S(1)}, u32[]{:S(2)}, u32[]{:S(2)}) %collective-permute-start.3) | collective-permute-done | bytes 196640 | tf_op jit(solution)/shard_map/while/body/eval_jaxpr/ppermute | solution.py:16
  46.7 6.1 %collective-permute-start.4 = (bf16[256,2048]{0,1:T(8,128)(2,1)}, bf16[256,2048]{0,1:T(8,128)(2,1)}, u32[]{:S(2)}, u32[]{:S(2)}) collective-permute-start(bf16[256,2048]{0,1:T(8,128)(2,1)} %bitcast.67), channel_id=1, source_target_pairs={{0,32},{32,64},{64,96},{96,128},{128,160},{160,192},{192,224},{1,3... | collective-permute-start | bytes 3145736 | tf_op jit(solution)/shard_map/while/body/eval_jaxpr/ppermute | solution.py:27
  55.1 12.8 %collective-permute-done.4 = bf16[256,2048]{0,1:T(8,128)(2,1)} collective-permute-done((bf16[256,2048]{0,1:T(8,128)(2,1)}, bf16[256,2048]{0,1:T(8,128)(2,1)}, u32[]{:S(2)}, u32[]{:S(2)}) %collective-permute-start.4) | collective-permute-done | bytes 1048608 | tf_op jit(solution)/shard_map/while/body/eval_jaxpr/ppermute | solution.py:27
  73.8 6.5 %collective-permute-done.1 = bf16[256,384]{0,1:T(8,128)(2,1)S(1)} collective-permute-done((bf16[256,384]{0,1:T(8,128)(2,1)S(1)}, bf16[256,384]{0,1:T(8,128)(2,1)S(1)}, u32[]{:S(2)}, u32[]{:S(2)}) %collective-permute-start.1) | collective-permute-done | bytes 196640 | tf_op jit(solution)/shard_map/while/body/eval_jaxpr/ppermute | solution.py:16
  85.3 5.7 %collective-permute-done.3 = bf16[256,384]{0,1:T(8,128)(2,1)S(1)} collective-permute-done((bf16[256,384]{0,1:T(8,128)(2,1)S(1)}, bf16[256,384]{0,1:T(8,128)(2,1)S(1)}, u32[]{:S(2)}, u32[]{:S(2)}) %collective-permute-start.3) | collective-permute-done | bytes 196640 | tf_op jit(solution)/shard_map/while/body/eval_jaxpr/ppermute | solution.py:16
  93.7 6.3 %collective-permute-start.4 = (bf16[256,2048]{0,1:T(8,128)(2,1)}, bf16[256,2048]{0,1:T(8,128)(2,1)}, u32[]{:S(2)}, u32[]{:S(2)}) collective-permute-start(bf16[256,2048]{0,1:T(8,128)(2,1)} %bitcast.67), channel_id=1, source_target_pairs={{0,32},{32,64},{64,96},{96,128},{128,160},{160,192},{192,224},{1,3... | collective-permute-start | bytes 3145736 | tf_op jit(solution)/shard_map/while/body/eval_jaxpr/ppermute | solution.py:27
  102.4 14.1 %collective-permute-done.4 = bf16[256,2048]{0,1:T(8,128)(2,1)} collective-permute-done((bf16[256,2048]{0,1:T(8,128)(2,1)}, bf16[256,2048]{0,1:T(8,128)(2,1)}, u32[]{:S(2)}, u32[]{:S(2)}) %collective-permute-start.4) | collective-permute-done | bytes 1048608 | tf_op jit(solution)/shard_map/while/body/eval_jaxpr/ppermute | solution.py:27
  140.6 6.6 %collective-permute-start.4 = (bf16[256,2048]{0,1:T(8,128)(2,1)}, bf16[256,2048]{0,1:T(8,128)(2,1)}, u32[]{:S(2)}, u32[]{:S(2)}) collective-permute-start(bf16[256,2048]{0,1:T(8,128)(2,1)} %bitcast.67), channel_id=1, source_target_pairs={{0,32},{32,64},{64,96},{96,128},{128,160},{160,192},{192,224},{1,3... | collective-permute-start | bytes 3145736 | tf_op jit(solution)/shard_map/while/body/eval_jaxpr/ppermute | solution.py:27
  149.6 14.1 %collective-permute-done.4 = bf16[256,2048]{0,1:T(8,128)(2,1)} collective-permute-done((bf16[256,2048]{0,1:T(8,128)(2,1)}, bf16[256,2048]{0,1:T(8,128)(2,1)}, u32[]{:S(2)}, u32[]{:S(2)}) %collective-permute-start.4) | collective-permute-done | bytes 1048608 | tf_op jit(solution)/shard_map/while/body/eval_jaxpr/ppermute | solution.py:27
  187.8 6.6 %collective-permute-start.4 = (bf16[256,2048]{0,1:T(8,128)(2,1)}, bf16[256,2048]{0,1:T(8,128)(2,1)}, u32[]{:S(2)}, u32[]{:S(2)}) collective-permute-start(bf16[256,2048]{0,1:T(8,128)(2,1)} %bitcast.67), channel_id=1, source_target_pairs={{0,32},{32,64},{64,96},{96,128},{128,160},{160,192},{192,224},{1,3... | collective-permute-start | bytes 3145736 | tf_op jit(solution)/shard_map/while/body/eval_jaxpr/ppermute | solution.py:27
  196.7 14.1 %collective-permute-done.4 = bf16[256,2048]{0,1:T(8,128)(2,1)} collective-permute-done((bf16[256,2048]{0,1:T(8,128)(2,1)}, bf16[256,2048]{0,1:T(8,128)(2,1)}, u32[]{:S(2)}, u32[]{:S(2)}) %collective-permute-start.4) | collective-permute-done | bytes 1048608 | tf_op jit(solution)/shard_map/while/body/eval_jaxpr/ppermute | solution.py:27
  234.9 7.3 %collective-permute-start.4 = (bf16[256,2048]{0,1:T(8,128)(2,1)}, bf16[256,2048]{0,1:T(8,128)(2,1)}, u32[]{:S(2)}, u32[]{:S(2)}) collective-permute-start(bf16[256,2048]{0,1:T(8,128)(2,1)} %bitcast.67), channel_id=1, source_target_pairs={{0,32},{32,64},{64,96},{96,128},{128,160},{160,192},{192,224},{1,3... | collective-permute-start | bytes 3145736 | tf_op jit(solution)/shard_map/while/body/eval_jaxpr/ppermute | solution.py:27
  244.6 14.1 %collective-permute-done.4 = bf16[256,2048]{0,1:T(8,128)(2,1)} collective-permute-done((bf16[256,2048]{0,1:T(8,128)(2,1)}, bf16[256,2048]{0,1:T(8,128)(2,1)}, u32[]{:S(2)}, u32[]{:S(2)}) %collective-permute-start.4) | collective-permute-done | bytes 1048608 | tf_op jit(solution)/shard_map/while/body/eval_jaxpr/ppermute | solution.py:27
  282.8 7.8 %collective-permute-start.4 = (bf16[256,2048]{0,1:T(8,128)(2,1)}, bf16[256,2048]{0,1:T(8,128)(2,1)}, u32[]{:S(2)}, u32[]{:S(2)}) collective-permute-start(bf16[256,2048]{0,1:T(8,128)(2,1)} %bitcast.67), channel_id=1, source_target_pairs={{0,32},{32,64},{64,96},{96,128},{128,160},{160,192},{192,224},{1,3... | collective-permute-start | bytes 3145736 | tf_op jit(solution)/shard_map/while/body/eval_jaxpr/ppermute | solution.py:27
  293.0 14.1 %collective-permute-done.4 = bf16[256,2048]{0,1:T(8,128)(2,1)} collective-permute-done((bf16[256,2048]{0,1:T(8,128)(2,1)}, bf16[256,2048]{0,1:T(8,128)(2,1)}, u32[]{:S(2)}, u32[]{:S(2)}) %collective-permute-start.4) | collective-permute-done | bytes 1048608 | tf_op jit(solution)/shard_map/while/body/eval_jaxpr/ppermute | solution.py:27
  331.2 7.8 %collective-permute-start.4 = (bf16[256,2048]{0,1:T(8,128)(2,1)}, bf16[256,2048]{0,1:T(8,128)(2,1)}, u32[]{:S(2)}, u32[]{:S(2)}) collective-permute-start(bf16[256,2048]{0,1:T(8,128)(2,1)} %bitcast.67), channel_id=1, source_target_pairs={{0,32},{32,64},{64,96},{96,128},{128,160},{160,192},{192,224},{1,3... | collective-permute-start | bytes 3145736 | tf_op jit(solution)/shard_map/while/body/eval_jaxpr/ppermute | solution.py:27
  341.4 14.1 %collective-permute-done.4 = bf16[256,2048]{0,1:T(8,128)(2,1)} collective-permute-done((bf16[256,2048]{0,1:T(8,128)(2,1)}, bf16[256,2048]{0,1:T(8,128)(2,1)}, u32[]{:S(2)}, u32[]{:S(2)}) %collective-permute-start.4) | collective-permute-done | bytes 1048608 | tf_op jit(solution)/shard_map/while/body/eval_jaxpr/ppermute | solution.py:27
  371.5 5.3 collective-permute-done.3
  379.6 7.8 %collective-permute-start.4 = (bf16[256,2048]{0,1:T(8,128)(2,1)}, bf16[256,2048]{0,1:T(8,128)(2,1)}, u32[]{:S(2)}, u32[]{:S(2)}) collective-permute-start(bf16[256,2048]{0,1:T(8,128)(2,1)} %bitcast.67), channel_id=1, source_target_pairs={{0,32},{32,64},{64,96},{96,128},{128,160},{160,192},{192,224},{1,3... | collective-permute-start | bytes 3145736 | tf_op jit(solution)/shard_map/while/body/eval_jaxpr/ppermute | solution.py:27
  389.8 14.1 %collective-permute-done.4 = bf16[256,2048]{0,1:T(8,128)(2,1)} collective-permute-done((bf16[256,2048]{0,1:T(8,128)(2,1)}, bf16[256,2048]{0,1:T(8,128)(2,1)}, u32[]{:S(2)}, u32[]{:S(2)}) %collective-permute-start.4) | collective-permute-done | bytes 1048608 | tf_op jit(solution)/shard_map/while/body/eval_jaxpr/ppermute | solution.py:27
  428.0 7.8 %collective-permute-start.4 = (bf16[256,2048]{0,1:T(8,128)(2,1)}, bf16[256,2048]{0,1:T(8,128)(2,1)}, u32[]{:S(2)}, u32[]{:S(2)}) collective-permute-start(bf16[256,2048]{0,1:T(8,128)(2,1)} %bitcast.67), channel_id=1, source_target_pairs={{0,32},{32,64},{64,96},{96,128},{128,160},{160,192},{192,224},{1,3... | collective-permute-start | bytes 3145736 | tf_op jit(solution)/shard_map/while/body/eval_jaxpr/ppermute | solution.py:27
  438.2 14.1 %collective-permute-done.4 = bf16[256,2048]{0,1:T(8,128)(2,1)} collective-permute-done((bf16[256,2048]{0,1:T(8,128)(2,1)}, bf16[256,2048]{0,1:T(8,128)(2,1)}, u32[]{:S(2)}, u32[]{:S(2)}) %collective-permute-start.4) | collective-permute-done | bytes 1048608 | tf_op jit(solution)/shard_map/while/body/eval_jaxpr/ppermute | solution.py:27
  453.8 90.2 %all-reduce.2.cloned.1.call-done = bf16[2,256,2048]{2,1,0:T(8,128)(2,1)} async-done(((bf16[2,256,2048]{2,1,0:T(8,128)(2,1)}), bf16[2,256,2048]{2,1,0:T(8,128)(2,1)}) %all-reduce.2.cloned.1.call-update) | async-done | bytes 2097168 | tf_op jit(solution)/shard_map/psum | solution.py:32
  (267 shorter events, 228.6 us)
Async XLA Ops:
  6.5 537.5 %all-reduce.2.cloned.1.call-start = ((), (), s32[]{:S(2)}) async-start(), calls=%async_computation | async-start | bytes 4194304 | tf_op jit(solution)/shard_map/psum | solution.py:32
  33.2 10.8 %collective-permute-start.3 = (bf16[256,384]{0,1:T(8,128)(2,1)S(1)}, bf16[256,384]{0,1:T(8,128)(2,1)S(1)}, u32[]{:S(2)}, u32[]{:S(2)}) collective-permute-start(bf16[256,384]{0,1:T(8,128)(2,1)S(1)} %get-tuple-element.419), channel_id=1, source_target_pairs={{0,1},{1,2},{2,3},{3,4},{4,5},{5,6},{6,7},{7,8},{8,9},{9,10},{10,1... | collective-permute-start | bytes 589832 | tf_op jit(solution)/shard_map/while/body/eval_jaxpr/ppermute | solution.py:16
  46.7 21.2 %collective-permute-start.4 = (bf16[256,2048]{0,1:T(8,128)(2,1)}, bf16[256,2048]{0,1:T(8,128)(2,1)}, u32[]{:S(2)}, u32[]{:S(2)}) collective-permute-start(bf16[256,2048]{0,1:T(8,128)(2,1)} %bitcast.67), channel_id=1, source_target_pairs={{0,32},{32,64},{64,96},{96,128},{128,160},{160,192},{192,224},{1,3... | collective-permute-start | bytes 3145736 | tf_op jit(solution)/shard_map/while/body/eval_jaxpr/ppermute | solution.py:27
  70.4 9.8 %collective-permute-start.1 = (bf16[256,384]{0,1:T(8,128)(2,1)S(1)}, bf16[256,384]{0,1:T(8,128)(2,1)S(1)}, u32[]{:S(2)}, u32[]{:S(2)}) collective-permute-start(bf16[256,384]{0,1:T(8,128)(2,1)S(1)} %get-tuple-element.411), channel_id=1, source_target_pairs={{0,1},{1,2},{2,3},{3,4},{4,5},{5,6},{6,7},{7,8},{8,9},{9,10},{10,1... | collective-permute-start | bytes 589832 | tf_op jit(solution)/shard_map/while/body/eval_jaxpr/ppermute | solution.py:16
  82.1 8.9 %collective-permute-start.3 = (bf16[256,384]{0,1:T(8,128)(2,1)S(1)}, bf16[256,384]{0,1:T(8,128)(2,1)S(1)}, u32[]{:S(2)}, u32[]{:S(2)}) collective-permute-start(bf16[256,384]{0,1:T(8,128)(2,1)S(1)} %get-tuple-element.419), channel_id=1, source_target_pairs={{0,1},{1,2},{2,3},{3,4},{4,5},{5,6},{6,7},{7,8},{8,9},{9,10},{10,1... | collective-permute-start | bytes 589832 | tf_op jit(solution)/shard_map/while/body/eval_jaxpr/ppermute | solution.py:16
  93.7 22.7 %collective-permute-start.4 = (bf16[256,2048]{0,1:T(8,128)(2,1)}, bf16[256,2048]{0,1:T(8,128)(2,1)}, u32[]{:S(2)}, u32[]{:S(2)}) collective-permute-start(bf16[256,2048]{0,1:T(8,128)(2,1)} %bitcast.67), channel_id=1, source_target_pairs={{0,32},{32,64},{64,96},{96,128},{128,160},{160,192},{192,224},{1,3... | collective-permute-start | bytes 3145736 | tf_op jit(solution)/shard_map/while/body/eval_jaxpr/ppermute | solution.py:27
  118.9 8.6 %collective-permute-start.1 = (bf16[256,384]{0,1:T(8,128)(2,1)S(1)}, bf16[256,384]{0,1:T(8,128)(2,1)S(1)}, u32[]{:S(2)}, u32[]{:S(2)}) collective-permute-start(bf16[256,384]{0,1:T(8,128)(2,1)S(1)} %get-tuple-element.411), channel_id=1, source_target_pairs={{0,1},{1,2},{2,3},{3,4},{4,5},{5,6},{6,7},{7,8},{8,9},{9,10},{10,1... | collective-permute-start | bytes 589832 | tf_op jit(solution)/shard_map/while/body/eval_jaxpr/ppermute | solution.py:16
  129.4 8.5 %collective-permute-start.3 = (bf16[256,384]{0,1:T(8,128)(2,1)S(1)}, bf16[256,384]{0,1:T(8,128)(2,1)S(1)}, u32[]{:S(2)}, u32[]{:S(2)}) collective-permute-start(bf16[256,384]{0,1:T(8,128)(2,1)S(1)} %get-tuple-element.419), channel_id=1, source_target_pairs={{0,1},{1,2},{2,3},{3,4},{4,5},{5,6},{6,7},{7,8},{8,9},{9,10},{10,1... | collective-permute-start | bytes 589832 | tf_op jit(solution)/shard_map/while/body/eval_jaxpr/ppermute | solution.py:16
  140.6 23.1 %collective-permute-start.4 = (bf16[256,2048]{0,1:T(8,128)(2,1)}, bf16[256,2048]{0,1:T(8,128)(2,1)}, u32[]{:S(2)}, u32[]{:S(2)}) collective-permute-start(bf16[256,2048]{0,1:T(8,128)(2,1)} %bitcast.67), channel_id=1, source_target_pairs={{0,32},{32,64},{64,96},{96,128},{128,160},{160,192},{192,224},{1,3... | collective-permute-start | bytes 3145736 | tf_op jit(solution)/shard_map/while/body/eval_jaxpr/ppermute | solution.py:27
  176.5 8.5 %collective-permute-start.3 = (bf16[256,384]{0,1:T(8,128)(2,1)S(1)}, bf16[256,384]{0,1:T(8,128)(2,1)S(1)}, u32[]{:S(2)}, u32[]{:S(2)}) collective-permute-start(bf16[256,384]{0,1:T(8,128)(2,1)S(1)} %get-tuple-element.419), channel_id=1, source_target_pairs={{0,1},{1,2},{2,3},{3,4},{4,5},{5,6},{6,7},{7,8},{8,9},{9,10},{10,1... | collective-permute-start | bytes 589832 | tf_op jit(solution)/shard_map/while/body/eval_jaxpr/ppermute | solution.py:16
  187.8 23.1 %collective-permute-start.4 = (bf16[256,2048]{0,1:T(8,128)(2,1)}, bf16[256,2048]{0,1:T(8,128)(2,1)}, u32[]{:S(2)}, u32[]{:S(2)}) collective-permute-start(bf16[256,2048]{0,1:T(8,128)(2,1)} %bitcast.67), channel_id=1, source_target_pairs={{0,32},{32,64},{64,96},{96,128},{128,160},{160,192},{192,224},{1,3... | collective-permute-start | bytes 3145736 | tf_op jit(solution)/shard_map/while/body/eval_jaxpr/ppermute | solution.py:27
  213.3 8.5 %collective-permute-start.1 = (bf16[256,384]{0,1:T(8,128)(2,1)S(1)}, bf16[256,384]{0,1:T(8,128)(2,1)S(1)}, u32[]{:S(2)}, u32[]{:S(2)}) collective-permute-start(bf16[256,384]{0,1:T(8,128)(2,1)S(1)} %get-tuple-element.411), channel_id=1, source_target_pairs={{0,1},{1,2},{2,3},{3,4},{4,5},{5,6},{6,7},{7,8},{8,9},{9,10},{10,1... | collective-permute-start | bytes 589832 | tf_op jit(solution)/shard_map/while/body/eval_jaxpr/ppermute | solution.py:16
  234.9 23.8 %collective-permute-start.4 = (bf16[256,2048]{0,1:T(8,128)(2,1)}, bf16[256,2048]{0,1:T(8,128)(2,1)}, u32[]{:S(2)}, u32[]{:S(2)}) collective-permute-start(bf16[256,2048]{0,1:T(8,128)(2,1)} %bitcast.67), channel_id=1, source_target_pairs={{0,32},{32,64},{64,96},{96,128},{128,160},{160,192},{192,224},{1,3... | collective-permute-start | bytes 3145736 | tf_op jit(solution)/shard_map/while/body/eval_jaxpr/ppermute | solution.py:27
  261.2 8.5 %collective-permute-start.1 = (bf16[256,384]{0,1:T(8,128)(2,1)S(1)}, bf16[256,384]{0,1:T(8,128)(2,1)S(1)}, u32[]{:S(2)}, u32[]{:S(2)}) collective-permute-start(bf16[256,384]{0,1:T(8,128)(2,1)S(1)} %get-tuple-element.411), channel_id=1, source_target_pairs={{0,1},{1,2},{2,3},{3,4},{4,5},{5,6},{6,7},{7,8},{8,9},{9,10},{10,1... | collective-permute-start | bytes 589832 | tf_op jit(solution)/shard_map/while/body/eval_jaxpr/ppermute | solution.py:16
  271.6 8.5 %collective-permute-start.3 = (bf16[256,384]{0,1:T(8,128)(2,1)S(1)}, bf16[256,384]{0,1:T(8,128)(2,1)S(1)}, u32[]{:S(2)}, u32[]{:S(2)}) collective-permute-start(bf16[256,384]{0,1:T(8,128)(2,1)S(1)} %get-tuple-element.419), channel_id=1, source_target_pairs={{0,1},{1,2},{2,3},{3,4},{4,5},{5,6},{6,7},{7,8},{8,9},{9,10},{10,1... | collective-permute-start | bytes 589832 | tf_op jit(solution)/shard_map/while/body/eval_jaxpr/ppermute | solution.py:16
  282.8 24.3 %collective-permute-start.4 = (bf16[256,2048]{0,1:T(8,128)(2,1)}, bf16[256,2048]{0,1:T(8,128)(2,1)}, u32[]{:S(2)}, u32[]{:S(2)}) collective-permute-start(bf16[256,2048]{0,1:T(8,128)(2,1)} %bitcast.67), channel_id=1, source_target_pairs={{0,32},{32,64},{64,96},{96,128},{128,160},{160,192},{192,224},{1,3... | collective-permute-start | bytes 3145736 | tf_op jit(solution)/shard_map/while/body/eval_jaxpr/ppermute | solution.py:27
  309.6 8.5 %collective-permute-start.1 = (bf16[256,384]{0,1:T(8,128)(2,1)S(1)}, bf16[256,384]{0,1:T(8,128)(2,1)S(1)}, u32[]{:S(2)}, u32[]{:S(2)}) collective-permute-start(bf16[256,384]{0,1:T(8,128)(2,1)S(1)} %get-tuple-element.411), channel_id=1, source_target_pairs={{0,1},{1,2},{2,3},{3,4},{4,5},{5,6},{6,7},{7,8},{8,9},{9,10},{10,1... | collective-permute-start | bytes 589832 | tf_op jit(solution)/shard_map/while/body/eval_jaxpr/ppermute | solution.py:16
  320.0 8.5 %collective-permute-start.3 = (bf16[256,384]{0,1:T(8,128)(2,1)S(1)}, bf16[256,384]{0,1:T(8,128)(2,1)S(1)}, u32[]{:S(2)}, u32[]{:S(2)}) collective-permute-start(bf16[256,384]{0,1:T(8,128)(2,1)S(1)} %get-tuple-element.419), channel_id=1, source_target_pairs={{0,1},{1,2},{2,3},{3,4},{4,5},{5,6},{6,7},{7,8},{8,9},{9,10},{10,1... | collective-permute-start | bytes 589832 | tf_op jit(solution)/shard_map/while/body/eval_jaxpr/ppermute | solution.py:16
  331.2 24.3 %collective-permute-start.4 = (bf16[256,2048]{0,1:T(8,128)(2,1)}, bf16[256,2048]{0,1:T(8,128)(2,1)}, u32[]{:S(2)}, u32[]{:S(2)}) collective-permute-start(bf16[256,2048]{0,1:T(8,128)(2,1)} %bitcast.67), channel_id=1, source_target_pairs={{0,32},{32,64},{64,96},{96,128},{128,160},{160,192},{192,224},{1,3... | collective-permute-start | bytes 3145736 | tf_op jit(solution)/shard_map/while/body/eval_jaxpr/ppermute | solution.py:27
  368.4 8.5 %collective-permute-start.3 = (bf16[256,384]{0,1:T(8,128)(2,1)S(1)}, bf16[256,384]{0,1:T(8,128)(2,1)S(1)}, u32[]{:S(2)}, u32[]{:S(2)}) collective-permute-start(bf16[256,384]{0,1:T(8,128)(2,1)S(1)} %get-tuple-element.419), channel_id=1, source_target_pairs={{0,1},{1,2},{2,3},{3,4},{4,5},{5,6},{6,7},{7,8},{8,9},{9,10},{10,1... | collective-permute-start | bytes 589832 | tf_op jit(solution)/shard_map/while/body/eval_jaxpr/ppermute | solution.py:16
  379.6 24.3 %collective-permute-start.4 = (bf16[256,2048]{0,1:T(8,128)(2,1)}, bf16[256,2048]{0,1:T(8,128)(2,1)}, u32[]{:S(2)}, u32[]{:S(2)}) collective-permute-start(bf16[256,2048]{0,1:T(8,128)(2,1)} %bitcast.67), channel_id=1, source_target_pairs={{0,32},{32,64},{64,96},{96,128},{128,160},{160,192},{192,224},{1,3... | collective-permute-start | bytes 3145736 | tf_op jit(solution)/shard_map/while/body/eval_jaxpr/ppermute | solution.py:27
  406.4 8.5 %collective-permute-start.1 = (bf16[256,384]{0,1:T(8,128)(2,1)S(1)}, bf16[256,384]{0,1:T(8,128)(2,1)S(1)}, u32[]{:S(2)}, u32[]{:S(2)}) collective-permute-start(bf16[256,384]{0,1:T(8,128)(2,1)S(1)} %get-tuple-element.411), channel_id=1, source_target_pairs={{0,1},{1,2},{2,3},{3,4},{4,5},{5,6},{6,7},{7,8},{8,9},{9,10},{10,1... | collective-permute-start | bytes 589832 | tf_op jit(solution)/shard_map/while/body/eval_jaxpr/ppermute | solution.py:16
  416.7 8.5 %collective-permute-start.3 = (bf16[256,384]{0,1:T(8,128)(2,1)S(1)}, bf16[256,384]{0,1:T(8,128)(2,1)S(1)}, u32[]{:S(2)}, u32[]{:S(2)}) collective-permute-start(bf16[256,384]{0,1:T(8,128)(2,1)S(1)} %get-tuple-element.419), channel_id=1, source_target_pairs={{0,1},{1,2},{2,3},{3,4},{4,5},{5,6},{6,7},{7,8},{8,9},{9,10},{10,1... | collective-permute-start | bytes 589832 | tf_op jit(solution)/shard_map/while/body/eval_jaxpr/ppermute | solution.py:16
  428.0 24.3 %collective-permute-start.4 = (bf16[256,2048]{0,1:T(8,128)(2,1)}, bf16[256,2048]{0,1:T(8,128)(2,1)}, u32[]{:S(2)}, u32[]{:S(2)}) collective-permute-start(bf16[256,2048]{0,1:T(8,128)(2,1)} %bitcast.67), channel_id=1, source_target_pairs={{0,32},{32,64},{64,96},{96,128},{128,160},{160,192},{192,224},{1,3... | collective-permute-start | bytes 3145736 | tf_op jit(solution)/shard_map/while/body/eval_jaxpr/ppermute | solution.py:27
  (22 other events, 92.1 us)
Sparse Core Ops, SparseCore 0:
  453.9 90.0 all-reduce.1
where the time goes:
time: 554 us; the launch traced here: 553 us
  waiting for transfers between devices  336 us (61%)
  local copies, waits for them, and re-layouts  78.1 us (14%)
  starting transfers between devices  74.7 us (13%)
  matrix products  34.4 us (6%)
  between operations  17.3 us (3%)
  other arithmetic  10.7 us (2%)
    ppermute x9, waiting for transfers between devices, from_behind(): lax.ppermute(value, axis, [(source, source + steps) for source in range(f...  126 us
    ppermute x18, waiting for transfers between devices, padded(): lax.ppermute(lax.slice_in_dim(block, block.shape[dim] - width, None, axis...  95.3 us
    psum x1, waiting for transfers between devices, spread(): return lax.psum(kept, axis)  90.2 us
    ppermute x9, starting transfers between devices, from_behind(): lax.ppermute(value, axis, [(source, source + steps) for source in range(f...  64.2 us
    dot_general x54, matrix products, apply_layer(): jnp.einsum('rjk,jkn->rjn', shifted, block_weights, preferred_element_type...  34.4 us
    ppermute x18, waiting for transfers between devices, padded(): lax.ppermute(lax.slice_in_dim(block, 0, width, axis=dim), axis, backward)  24.7 us
    squeeze x9, local copies, waits for them, and re-layouts, apply_layer(): layer_weights = table[layer, first:first + out_blocks]  22.4 us
    dynamic_slice x18, local copies, waits for them, and re-layouts, advance(): lax.dynamic_index_in_dim(finished_rows, slot_index, 0, keepdims=False)  19.7 us
  transfers between devices with their start and end apart: 46, of which 37 were waited for; matrix products, arithmetic and copies ran while one was open for 8% of the time, Pallas kernels for 0%

commit v1 on v0

--- a/solution.py
+++ b/solution.py
@@ -29,7 +29,7 @@
 
 def spread(value, axis, source):
     kept = jnp.where(lax.axis_index(axis) == source, value, 0).astype(value.dtype)
-    return lax.psum(kept, axis)
+    return jnp.sum(lax.all_gather(kept, axis), axis=0)
 
 
 def shards(inputs, weights, bias, offsets):

time: 554 us -> 655 us (1.18)
  waiting for transfers between devices: 336 us -> 427 us
  other arithmetic: 10.7 us -> 20.2 us
    all_gather x0 -> x1, waiting for transfers between devices: none -> 181 us  [spread(): return jnp.sum(lax.all_gather(kept, axis), axis=0)]
    psum x1 -> x0, waiting for transfers between devices: 90.2 us -> none  [spread(): return lax.psum(kept, axis)]
    reduce_sum x0 -> x1, other arithmetic: none -> 9.47 us  [spread(): return jnp.sum(lax.all_gather(kept, axis), axis=0)]
  transfers between devices with their start and end apart: 46 -> 46, of which waited for: 37 -> 37; matrix products, arithmetic and copies ran while one was open for 8% -> 7% of each run, Pallas kernels for 0% -> 0%
where the time goes in v1:
time: 655 us; the launch traced here: 653 us
  waiting for transfers between devices  427 us (65%)
  local copies, waits for them, and re-layouts  77.2 us (12%)
  starting transfers between devices  74.7 us (11%)
  matrix products  35 us (5%)
  other arithmetic  20.2 us (3%)
  between operations  17.2 us (3%)
    all_gather x1, waiting for transfers between devices, spread(): return jnp.sum(lax.all_gather(kept, axis), axis=0)  181 us
    ppermute x9, waiting for transfers between devices, from_behind(): lax.ppermute(value, axis, [(source, source + steps) for source in range(f...  126 us
    ppermute x18, waiting for transfers between devices, padded(): lax.ppermute(lax.slice_in_dim(block, block.shape[dim] - width, None, axis...  95.3 us
    ppermute x9, starting transfers between devices, from_behind(): lax.ppermute(value, axis, [(source, source + steps) for source in range(f...  64.2 us
    dot_general x54, matrix products, apply_layer(): jnp.einsum('rjk,jkn->rjn', shifted, block_weights, preferred_element_type...  35 us
    ppermute x18, waiting for transfers between devices, padded(): lax.ppermute(lax.slice_in_dim(block, 0, width, axis=dim), axis, backward)  24.7 us
    squeeze x9, local copies, waits for them, and re-layouts, apply_layer(): layer_weights = table[layer, first:first + out_blocks]  22.4 us
    dynamic_slice x18, local copies, waits for them, and re-layouts, advance(): lax.dynamic_index_in_dim(finished_rows, slot_index, 0, keepdims=False)  19.7 us
  transfers between devices with their start and end apart: 46, of which 37 were waited for; matrix products, arithmetic and copies ran while one was open for 7% of the time, Pallas kernels for 0%

profile of v1, /device:TPU:2, one launch (start us, length us, event | category | flops | bytes accessed | tf_op | source)
XLA Modules:
  0.0 652.6 jit_solution(5940776619914190668)
XLA Ops:
  22.5 430.3 %while.17 = (s32[]{:T(128)}, bf16[256,2048]{0,1:T(8,128)(2,1)}, bf16[2,256,2048]{2,1,0:T(8,128)(2,1)}, pred[]{:T(512)}, bf16[2,256,2048]{2,1,0:T(8,128)(2,1)}, /...) while((s32[]{:T(128)}, bf16[256,2048]{0,1:T(8,128)(2,1)}, ...), condition=%wide.region_1.2_spmd, body=%wide.region_0.1_spmd.sunk | while | flops 820252672 | bytes 80798200 | solution.py:107
  36.3 7.6 %collective-permute-done.3 = bf16[256,384]{0,1:T(8,128)(2,1)S(1)} collective-permute-done((bf16[256,384]{0,1:T(8,128)(2,1)S(1)}, bf16[256,384]{0,1:T(8,128)(2,1)S(1)}, u32[]{:S(2)}, u32[]{:S(2)}) %collective-permute-start.3) | collective-permute-done | bytes 196640 | tf_op jit(solution)/shard_map/while/body/eval_jaxpr/ppermute | solution.py:16
  46.7 6.0 collective-permute-start.4
  55.1 12.8 %collective-permute-done.4 = bf16[256,2048]{0,1:T(8,128)(2,1)} collective-permute-done((bf16[256,2048]{0,1:T(8,128)(2,1)}, bf16[256,2048]{0,1:T(8,128)(2,1)}, u32[]{:S(2)}, u32[]{:S(2)}) %collective-permute-start.4) | collective-permute-done | bytes 1048608 | tf_op jit(solution)/shard_map/while/body/eval_jaxpr/ppermute | solution.py:27
  73.8 6.5 collective-permute-done.1
  85.3 5.7 collective-permute-done.3
  93.8 6.3 collective-permute-start.4
  102.4 14.1 %collective-permute-done.4 = bf16[256,2048]{0,1:T(8,128)(2,1)} collective-permute-done((bf16[256,2048]{0,1:T(8,128)(2,1)}, bf16[256,2048]{0,1:T(8,128)(2,1)}, u32[]{:S(2)}, u32[]{:S(2)}) %collective-permute-start.4) | collective-permute-done | bytes 1048608 | tf_op jit(solution)/shard_map/while/body/eval_jaxpr/ppermute | solution.py:27
  140.7 6.6 %collective-permute-start.4 = (bf16[256,2048]{0,1:T(8,128)(2,1)}, bf16[256,2048]{0,1:T(8,128)(2,1)}, u32[]{:S(2)}, u32[]{:S(2)}) collective-permute-start(bf16[256,2048]{0,1:T(8,128)(2,1)} %bitcast.68), channel_id=1, source_target_pairs={{0,32},{32,64},{64,96},{96,128},{128,160},{160,192},{192,224},{1,3... | collective-permute-start | bytes 3145736 | tf_op jit(solution)/shard_map/while/body/eval_jaxpr/ppermute | solution.py:27
  149.7 14.1 %collective-permute-done.4 = bf16[256,2048]{0,1:T(8,128)(2,1)} collective-permute-done((bf16[256,2048]{0,1:T(8,128)(2,1)}, bf16[256,2048]{0,1:T(8,128)(2,1)}, u32[]{:S(2)}, u32[]{:S(2)}) %collective-permute-start.4) | collective-permute-done | bytes 1048608 | tf_op jit(solution)/shard_map/while/body/eval_jaxpr/ppermute | solution.py:27
  188.0 6.6 %collective-permute-start.4 = (bf16[256,2048]{0,1:T(8,128)(2,1)}, bf16[256,2048]{0,1:T(8,128)(2,1)}, u32[]{:S(2)}, u32[]{:S(2)}) collective-permute-start(bf16[256,2048]{0,1:T(8,128)(2,1)} %bitcast.68), channel_id=1, source_target_pairs={{0,32},{32,64},{64,96},{96,128},{128,160},{160,192},{192,224},{1,3... | collective-permute-start | bytes 3145736 | tf_op jit(solution)/shard_map/while/body/eval_jaxpr/ppermute | solution.py:27
  196.9 14.1 %collective-permute-done.4 = bf16[256,2048]{0,1:T(8,128)(2,1)} collective-permute-done((bf16[256,2048]{0,1:T(8,128)(2,1)}, bf16[256,2048]{0,1:T(8,128)(2,1)}, u32[]{:S(2)}, u32[]{:S(2)}) %collective-permute-start.4) | collective-permute-done | bytes 1048608 | tf_op jit(solution)/shard_map/while/body/eval_jaxpr/ppermute | solution.py:27
  235.2 7.4 %collective-permute-start.4 = (bf16[256,2048]{0,1:T(8,128)(2,1)}, bf16[256,2048]{0,1:T(8,128)(2,1)}, u32[]{:S(2)}, u32[]{:S(2)}) collective-permute-start(bf16[256,2048]{0,1:T(8,128)(2,1)} %bitcast.68), channel_id=1, source_target_pairs={{0,32},{32,64},{64,96},{96,128},{128,160},{160,192},{192,224},{1,3... | collective-permute-start | bytes 3145736 | tf_op jit(solution)/shard_map/while/body/eval_jaxpr/ppermute | solution.py:27
  244.9 14.1 %collective-permute-done.4 = bf16[256,2048]{0,1:T(8,128)(2,1)} collective-permute-done((bf16[256,2048]{0,1:T(8,128)(2,1)}, bf16[256,2048]{0,1:T(8,128)(2,1)}, u32[]{:S(2)}, u32[]{:S(2)}) %collective-permute-start.4) | collective-permute-done | bytes 1048608 | tf_op jit(solution)/shard_map/while/body/eval_jaxpr/ppermute | solution.py:27
  283.2 7.8 %collective-permute-start.4 = (bf16[256,2048]{0,1:T(8,128)(2,1)}, bf16[256,2048]{0,1:T(8,128)(2,1)}, u32[]{:S(2)}, u32[]{:S(2)}) collective-permute-start(bf16[256,2048]{0,1:T(8,128)(2,1)} %bitcast.68), channel_id=1, source_target_pairs={{0,32},{32,64},{64,96},{96,128},{128,160},{160,192},{192,224},{1,3... | collective-permute-start | bytes 3145736 | tf_op jit(solution)/shard_map/while/body/eval_jaxpr/ppermute | solution.py:27
  293.3 14.1 %collective-permute-done.4 = bf16[256,2048]{0,1:T(8,128)(2,1)} collective-permute-done((bf16[256,2048]{0,1:T(8,128)(2,1)}, bf16[256,2048]{0,1:T(8,128)(2,1)}, u32[]{:S(2)}, u32[]{:S(2)}) %collective-permute-start.4) | collective-permute-done | bytes 1048608 | tf_op jit(solution)/shard_map/while/body/eval_jaxpr/ppermute | solution.py:27
  331.6 7.8 %collective-permute-start.4 = (bf16[256,2048]{0,1:T(8,128)(2,1)}, bf16[256,2048]{0,1:T(8,128)(2,1)}, u32[]{:S(2)}, u32[]{:S(2)}) collective-permute-start(bf16[256,2048]{0,1:T(8,128)(2,1)} %bitcast.68), channel_id=1, source_target_pairs={{0,32},{32,64},{64,96},{96,128},{128,160},{160,192},{192,224},{1,3... | collective-permute-start | bytes 3145736 | tf_op jit(solution)/shard_map/while/body/eval_jaxpr/ppermute | solution.py:27
  341.8 14.1 %collective-permute-done.4 = bf16[256,2048]{0,1:T(8,128)(2,1)} collective-permute-done((bf16[256,2048]{0,1:T(8,128)(2,1)}, bf16[256,2048]{0,1:T(8,128)(2,1)}, u32[]{:S(2)}, u32[]{:S(2)}) %collective-permute-start.4) | collective-permute-done | bytes 1048608 | tf_op jit(solution)/shard_map/while/body/eval_jaxpr/ppermute | solution.py:27
  380.1 7.8 %collective-permute-start.4 = (bf16[256,2048]{0,1:T(8,128)(2,1)}, bf16[256,2048]{0,1:T(8,128)(2,1)}, u32[]{:S(2)}, u32[]{:S(2)}) collective-permute-start(bf16[256,2048]{0,1:T(8,128)(2,1)} %bitcast.68), channel_id=1, source_target_pairs={{0,32},{32,64},{64,96},{96,128},{128,160},{160,192},{192,224},{1,3... | collective-permute-start | bytes 3145736 | tf_op jit(solution)/shard_map/while/body/eval_jaxpr/ppermute | solution.py:27
  390.2 14.1 %collective-permute-done.4 = bf16[256,2048]{0,1:T(8,128)(2,1)} collective-permute-done((bf16[256,2048]{0,1:T(8,128)(2,1)}, bf16[256,2048]{0,1:T(8,128)(2,1)}, u32[]{:S(2)}, u32[]{:S(2)}) %collective-permute-start.4) | collective-permute-done | bytes 1048608 | tf_op jit(solution)/shard_map/while/body/eval_jaxpr/ppermute | solution.py:27
  428.5 7.8 %collective-permute-start.4 = (bf16[256,2048]{0,1:T(8,128)(2,1)}, bf16[256,2048]{0,1:T(8,128)(2,1)}, u32[]{:S(2)}, u32[]{:S(2)}) collective-permute-start(bf16[256,2048]{0,1:T(8,128)(2,1)} %bitcast.68), channel_id=1, source_target_pairs={{0,32},{32,64},{64,96},{96,128},{128,160},{160,192},{192,224},{1,3... | collective-permute-start | bytes 3145736 | tf_op jit(solution)/shard_map/while/body/eval_jaxpr/ppermute | solution.py:27
  438.7 14.1 %collective-permute-done.4 = bf16[256,2048]{0,1:T(8,128)(2,1)} collective-permute-done((bf16[256,2048]{0,1:T(8,128)(2,1)}, bf16[256,2048]{0,1:T(8,128)(2,1)}, u32[]{:S(2)}, u32[]{:S(2)}) %collective-permute-start.4) | collective-permute-done | bytes 1048608 | tf_op jit(solution)/shard_map/while/body/eval_jaxpr/ppermute | solution.py:27
  454.4 181.2 %all-gather.3.cloned.1.call-done = bf16[16,256,2048]{2,1,0:T(8,128)(2,1)} async-done(((bf16[2,256,2048]{2,1,0:T(8,128)(2,1)}), bf16[16,256,2048]{2,1,0:T(8,128)(2,1)}) %all-gather.3.cloned.1.call-update) | async-done | bytes 16777232 | tf_op jit(solution)/shard_map/all_gather | solution.py:32
  635.5 9.5 %reduce_sum.12 = bf16[2,256,2048]{2,1,0:T(8,128)(2,1)S(1)} reduce(bf16[8,2,256,2048]{3,2,1,0:T(8,128)(2,1)} %bitcast.78, bf16[]{:T(256)} %constant.125.clone.1), dimensions={0}, to_apply=%region_2.3 | reduce | flops 7340032 | bytes 18874370 | tf_op jit(solution)/shard_map/reduce_sum | solution.py:32
  (268 shorter events, 233.5 us)
Async XLA Ops:
  6.5 629.0 %all-gather.3.cloned.1.call-start = ((), (), s32[]{:S(2)}) async-start(), calls=%async_computation | async-start | bytes 18874368 | tf_op jit(solution)/shard_map/all_gather | solution.py:32
  33.1 10.8 %collective-permute-start.3 = (bf16[256,384]{0,1:T(8,128)(2,1)S(1)}, bf16[256,384]{0,1:T(8,128)(2,1)S(1)}, u32[]{:S(2)}, u32[]{:S(2)}) collective-permute-start(bf16[256,384]{0,1:T(8,128)(2,1)S(1)} %get-tuple-element.432), channel_id=1, source_target_pairs={{0,1},{1,2},{2,3},{3,4},{4,5},{5,6},{6,7},{7,8},{8,9},{9,10},{10,1... | collective-permute-start | bytes 589832 | tf_op jit(solution)/shard_map/while/body/eval_jaxpr/ppermute | solution.py:16
  46.7 21.2 %collective-permute-start.4 = (bf16[256,2048]{0,1:T(8,128)(2,1)}, bf16[256,2048]{0,1:T(8,128)(2,1)}, u32[]{:S(2)}, u32[]{:S(2)}) collective-permute-start(bf16[256,2048]{0,1:T(8,128)(2,1)} %bitcast.68), channel_id=1, source_target_pairs={{0,32},{32,64},{64,96},{96,128},{128,160},{160,192},{192,224},{1,3... | collective-permute-start | bytes 3145736 | tf_op jit(solution)/shard_map/while/body/eval_jaxpr/ppermute | solution.py:27
  70.4 9.8 %collective-permute-start.1 = (bf16[256,384]{0,1:T(8,128)(2,1)S(1)}, bf16[256,384]{0,1:T(8,128)(2,1)S(1)}, u32[]{:S(2)}, u32[]{:S(2)}) collective-permute-start(bf16[256,384]{0,1:T(8,128)(2,1)S(1)} %get-tuple-element.424), channel_id=1, source_target_pairs={{0,1},{1,2},{2,3},{3,4},{4,5},{5,6},{6,7},{7,8},{8,9},{9,10},{10,1... | collective-permute-start | bytes 589832 | tf_op jit(solution)/shard_map/while/body/eval_jaxpr/ppermute | solution.py:16
  82.1 8.9 %collective-permute-start.3 = (bf16[256,384]{0,1:T(8,128)(2,1)S(1)}, bf16[256,384]{0,1:T(8,128)(2,1)S(1)}, u32[]{:S(2)}, u32[]{:S(2)}) collective-permute-start(bf16[256,384]{0,1:T(8,128)(2,1)S(1)} %get-tuple-element.432), channel_id=1, source_target_pairs={{0,1},{1,2},{2,3},{3,4},{4,5},{5,6},{6,7},{7,8},{8,9},{9,10},{10,1... | collective-permute-start | bytes 589832 | tf_op jit(solution)/shard_map/while/body/eval_jaxpr/ppermute | solution.py:16
  93.8 22.7 %collective-permute-start.4 = (bf16[256,2048]{0,1:T(8,128)(2,1)}, bf16[256,2048]{0,1:T(8,128)(2,1)}, u32[]{:S(2)}, u32[]{:S(2)}) collective-permute-start(bf16[256,2048]{0,1:T(8,128)(2,1)} %bitcast.68), channel_id=1, source_target_pairs={{0,32},{32,64},{64,96},{96,128},{128,160},{160,192},{192,224},{1,3... | collective-permute-start | bytes 3145736 | tf_op jit(solution)/shard_map/while/body/eval_jaxpr/ppermute | solution.py:27
  119.0 8.6 %collective-permute-start.1 = (bf16[256,384]{0,1:T(8,128)(2,1)S(1)}, bf16[256,384]{0,1:T(8,128)(2,1)S(1)}, u32[]{:S(2)}, u32[]{:S(2)}) collective-permute-start(bf16[256,384]{0,1:T(8,128)(2,1)S(1)} %get-tuple-element.424), channel_id=1, source_target_pairs={{0,1},{1,2},{2,3},{3,4},{4,5},{5,6},{6,7},{7,8},{8,9},{9,10},{10,1... | collective-permute-start | bytes 589832 | tf_op jit(solution)/shard_map/while/body/eval_jaxpr/ppermute | solution.py:16
  129.4 8.5 %collective-permute-start.3 = (bf16[256,384]{0,1:T(8,128)(2,1)S(1)}, bf16[256,384]{0,1:T(8,128)(2,1)S(1)}, u32[]{:S(2)}, u32[]{:S(2)}) collective-permute-start(bf16[256,384]{0,1:T(8,128)(2,1)S(1)} %get-tuple-element.432), channel_id=1, source_target_pairs={{0,1},{1,2},{2,3},{3,4},{4,5},{5,6},{6,7},{7,8},{8,9},{9,10},{10,1... | collective-permute-start | bytes 589832 | tf_op jit(solution)/shard_map/while/body/eval_jaxpr/ppermute | solution.py:16
  140.7 23.1 %collective-permute-start.4 = (bf16[256,2048]{0,1:T(8,128)(2,1)}, bf16[256,2048]{0,1:T(8,128)(2,1)}, u32[]{:S(2)}, u32[]{:S(2)}) collective-permute-start(bf16[256,2048]{0,1:T(8,128)(2,1)} %bitcast.68), channel_id=1, source_target_pairs={{0,32},{32,64},{64,96},{96,128},{128,160},{160,192},{192,224},{1,3... | collective-permute-start | bytes 3145736 | tf_op jit(solution)/shard_map/while/body/eval_jaxpr/ppermute | solution.py:27
  166.3 8.5 %collective-permute-start.1 = (bf16[256,384]{0,1:T(8,128)(2,1)S(1)}, bf16[256,384]{0,1:T(8,128)(2,1)S(1)}, u32[]{:S(2)}, u32[]{:S(2)}) collective-permute-start(bf16[256,384]{0,1:T(8,128)(2,1)S(1)} %get-tuple-element.424), channel_id=1, source_target_pairs={{0,1},{1,2},{2,3},{3,4},{4,5},{5,6},{6,7},{7,8},{8,9},{9,10},{10,1... | collective-permute-start | bytes 589832 | tf_op jit(solution)/shard_map/while/body/eval_jaxpr/ppermute | solution.py:16
  176.7 8.5 %collective-permute-start.3 = (bf16[256,384]{0,1:T(8,128)(2,1)S(1)}, bf16[256,384]{0,1:T(8,128)(2,1)S(1)}, u32[]{:S(2)}, u32[]{:S(2)}) collective-permute-start(bf16[256,384]{0,1:T(8,128)(2,1)S(1)} %get-tuple-element.432), channel_id=1, source_target_pairs={{0,1},{1,2},{2,3},{3,4},{4,5},{5,6},{6,7},{7,8},{8,9},{9,10},{10,1... | collective-permute-start | bytes 589832 | tf_op jit(solution)/shard_map/while/body/eval_jaxpr/ppermute | solution.py:16
  188.0 23.1 %collective-permute-start.4 = (bf16[256,2048]{0,1:T(8,128)(2,1)}, bf16[256,2048]{0,1:T(8,128)(2,1)}, u32[]{:S(2)}, u32[]{:S(2)}) collective-permute-start(bf16[256,2048]{0,1:T(8,128)(2,1)} %bitcast.68), channel_id=1, source_target_pairs={{0,32},{32,64},{64,96},{96,128},{128,160},{160,192},{192,224},{1,3... | collective-permute-start | bytes 3145736 | tf_op jit(solution)/shard_map/while/body/eval_jaxpr/ppermute | solution.py:27
  213.5 8.5 %collective-permute-start.1 = (bf16[256,384]{0,1:T(8,128)(2,1)S(1)}, bf16[256,384]{0,1:T(8,128)(2,1)S(1)}, u32[]{:S(2)}, u32[]{:S(2)}) collective-permute-start(bf16[256,384]{0,1:T(8,128)(2,1)S(1)} %get-tuple-element.424), channel_id=1, source_target_pairs={{0,1},{1,2},{2,3},{3,4},{4,5},{5,6},{6,7},{7,8},{8,9},{9,10},{10,1... | collective-permute-start | bytes 589832 | tf_op jit(solution)/shard_map/while/body/eval_jaxpr/ppermute | solution.py:16
  223.9 8.5 %collective-permute-start.3 = (bf16[256,384]{0,1:T(8,128)(2,1)S(1)}, bf16[256,384]{0,1:T(8,128)(2,1)S(1)}, u32[]{:S(2)}, u32[]{:S(2)}) collective-permute-start(bf16[256,384]{0,1:T(8,128)(2,1)S(1)} %get-tuple-element.432), channel_id=1, source_target_pairs={{0,1},{1,2},{2,3},{3,4},{4,5},{5,6},{6,7},{7,8},{8,9},{9,10},{10,1... | collective-permute-start | bytes 589832 | tf_op jit(solution)/shard_map/while/body/eval_jaxpr/ppermute | solution.py:16
  235.2 23.8 %collective-permute-start.4 = (bf16[256,2048]{0,1:T(8,128)(2,1)}, bf16[256,2048]{0,1:T(8,128)(2,1)}, u32[]{:S(2)}, u32[]{:S(2)}) collective-permute-start(bf16[256,2048]{0,1:T(8,128)(2,1)} %bitcast.68), channel_id=1, source_target_pairs={{0,32},{32,64},{64,96},{96,128},{128,160},{160,192},{192,224},{1,3... | collective-permute-start | bytes 3145736 | tf_op jit(solution)/shard_map/while/body/eval_jaxpr/ppermute | solution.py:27
  261.5 8.5 %collective-permute-start.1 = (bf16[256,384]{0,1:T(8,128)(2,1)S(1)}, bf16[256,384]{0,1:T(8,128)(2,1)S(1)}, u32[]{:S(2)}, u32[]{:S(2)}) collective-permute-start(bf16[256,384]{0,1:T(8,128)(2,1)S(1)} %get-tuple-element.424), channel_id=1, source_target_pairs={{0,1},{1,2},{2,3},{3,4},{4,5},{5,6},{6,7},{7,8},{8,9},{9,10},{10,1... | collective-permute-start | bytes 589832 | tf_op jit(solution)/shard_map/while/body/eval_jaxpr/ppermute | solution.py:16
  271.9 8.5 %collective-permute-start.3 = (bf16[256,384]{0,1:T(8,128)(2,1)S(1)}, bf16[256,384]{0,1:T(8,128)(2,1)S(1)}, u32[]{:S(2)}, u32[]{:S(2)}) collective-permute-start(bf16[256,384]{0,1:T(8,128)(2,1)S(1)} %get-tuple-element.432), channel_id=1, source_target_pairs={{0,1},{1,2},{2,3},{3,4},{4,5},{5,6},{6,7},{7,8},{8,9},{9,10},{10,1... | collective-permute-start | bytes 589832 | tf_op jit(solution)/shard_map/while/body/eval_jaxpr/ppermute | solution.py:16
  283.2 24.3 %collective-permute-start.4 = (bf16[256,2048]{0,1:T(8,128)(2,1)}, bf16[256,2048]{0,1:T(8,128)(2,1)}, u32[]{:S(2)}, u32[]{:S(2)}) collective-permute-start(bf16[256,2048]{0,1:T(8,128)(2,1)} %bitcast.68), channel_id=1, source_target_pairs={{0,32},{32,64},{64,96},{96,128},{128,160},{160,192},{192,224},{1,3... | collective-permute-start | bytes 3145736 | tf_op jit(solution)/shard_map/while/body/eval_jaxpr/ppermute | solution.py:27
  320.3 8.5 %collective-permute-start.3 = (bf16[256,384]{0,1:T(8,128)(2,1)S(1)}, bf16[256,384]{0,1:T(8,128)(2,1)S(1)}, u32[]{:S(2)}, u32[]{:S(2)}) collective-permute-start(bf16[256,384]{0,1:T(8,128)(2,1)S(1)} %get-tuple-element.432), channel_id=1, source_target_pairs={{0,1},{1,2},{2,3},{3,4},{4,5},{5,6},{6,7},{7,8},{8,9},{9,10},{10,1... | collective-permute-start | bytes 589832 | tf_op jit(solution)/shard_map/while/body/eval_jaxpr/ppermute | solution.py:16
  331.6 24.3 %collective-permute-start.4 = (bf16[256,2048]{0,1:T(8,128)(2,1)}, bf16[256,2048]{0,1:T(8,128)(2,1)}, u32[]{:S(2)}, u32[]{:S(2)}) collective-permute-start(bf16[256,2048]{0,1:T(8,128)(2,1)} %bitcast.68), channel_id=1, source_target_pairs={{0,32},{32,64},{64,96},{96,128},{128,160},{160,192},{192,224},{1,3... | collective-permute-start | bytes 3145736 | tf_op jit(solution)/shard_map/while/body/eval_jaxpr/ppermute | solution.py:27
  368.8 8.5 %collective-permute-start.3 = (bf16[256,384]{0,1:T(8,128)(2,1)S(1)}, bf16[256,384]{0,1:T(8,128)(2,1)S(1)}, u32[]{:S(2)}, u32[]{:S(2)}) collective-permute-start(bf16[256,384]{0,1:T(8,128)(2,1)S(1)} %get-tuple-element.432), channel_id=1, source_target_pairs={{0,1},{1,2},{2,3},{3,4},{4,5},{5,6},{6,7},{7,8},{8,9},{9,10},{10,1... | collective-permute-start | bytes 589832 | tf_op jit(solution)/shard_map/while/body/eval_jaxpr/ppermute | solution.py:16
  380.1 24.3 %collective-permute-start.4 = (bf16[256,2048]{0,1:T(8,128)(2,1)}, bf16[256,2048]{0,1:T(8,128)(2,1)}, u32[]{:S(2)}, u32[]{:S(2)}) collective-permute-start(bf16[256,2048]{0,1:T(8,128)(2,1)} %bitcast.68), channel_id=1, source_target_pairs={{0,32},{32,64},{64,96},{96,128},{128,160},{160,192},{192,224},{1,3... | collective-permute-start | bytes 3145736 | tf_op jit(solution)/shard_map/while/body/eval_jaxpr/ppermute | solution.py:27
  417.2 8.5 %collective-permute-start.3 = (bf16[256,384]{0,1:T(8,128)(2,1)S(1)}, bf16[256,384]{0,1:T(8,128)(2,1)S(1)}, u32[]{:S(2)}, u32[]{:S(2)}) collective-permute-start(bf16[256,384]{0,1:T(8,128)(2,1)S(1)} %get-tuple-element.432), channel_id=1, source_target_pairs={{0,1},{1,2},{2,3},{3,4},{4,5},{5,6},{6,7},{7,8},{8,9},{9,10},{10,1... | collective-permute-start | bytes 589832 | tf_op jit(solution)/shard_map/while/body/eval_jaxpr/ppermute | solution.py:16
  428.5 24.3 %collective-permute-start.4 = (bf16[256,2048]{0,1:T(8,128)(2,1)}, bf16[256,2048]{0,1:T(8,128)(2,1)}, u32[]{:S(2)}, u32[]{:S(2)}) collective-permute-start(bf16[256,2048]{0,1:T(8,128)(2,1)} %bitcast.68), channel_id=1, source_target_pairs={{0,32},{32,64},{64,96},{96,128},{128,160},{160,192},{192,224},{1,3... | collective-permute-start | bytes 3145736 | tf_op jit(solution)/shard_map/while/body/eval_jaxpr/ppermute | solution.py:27
  (22 other events, 92.1 us)
Sparse Core Ops, SparseCore 0:
  454.5 181.0 all-gather.2
